TPU v7x, 32 devices: a whole 2x2x4 slice. The times are simulated.
32 devices in a mesh: groups: 2 (over y), seq: 4 (over z), strand: 2 (over core), chan: 2 (over x).
Axes of the slice: x: 2, y: 2, z: 4, core: 2. Of those that a mesh axis runs over, the one named last changes fastest.
Arguments:
- seq_in: bfloat16 [2, 6144, 512], P('strand', ('groups', 'seq', 'chan')), parts along dimension 1, may hold values from -6 to 6
- conv_norm: float32 [2, 512], replicated, may hold values from 0.1 to 1.9
- conv_weight: bfloat16 [2, 3, 512, 512], P(None, None, None, ('seq', 'chan')), may hold values from -0.15625 to 0.15625
- ff_norm: float32 [2, 512], replicated, may hold values from 0.1 to 1.9
- up_weight: bfloat16 [2, 512, 2048], P(None, None, ('seq', 'chan')), may hold values from -0.25 to 0.25
- down_weight: bfloat16 [2, 2048, 512], P(None, ('seq', 'chan')), may hold values from -0.125 to 0.125
- head_norm: float32 [512], replicated, may hold values from 0.1 to 1.9
- value_weight: bfloat16 [512, 512], replicated, may hold values from -0.25 to 0.25
- gate_weight: bfloat16 [512, 512], replicated, may hold values from -0.25 to 0.25
- out_weight: bfloat16 [512, 512], replicated, may hold values from -0.25 to 0.25
Outputs:
- strand_out: bfloat16 [2, 6144, 512], P('strand', ('groups', 'seq', 'chan')), parts along dimension 1
There are 2 independent parts, one for each index of `groups`. A program takes and returns all parts, laid end to end along the dimension named above; an argument that names none is the same for every part. Nothing has to cross between parts.
All inputs are finite; a program needn't handle non-finite values.
Results may differ from a plain program's by a relative error of at most 0.015.
Values may be sent and summed in bfloat16 or wider, within the bound.
No kernel may reach another device: no remote copies, remote signals or barrier semaphores. Data moves between devices by JAX's collectives and lax.ppermute only.
A program may use at most 64 MiB of HBM per device.

v0:
```python
import jax
import jax.numpy as jnp
from jax import lax
from jax.sharding import PartitionSpec as P


def passed_along(value, axis, steps):
    count = lax.axis_size(axis)
    initial, last = (max(0, -steps), min(count, count - steps))
    return lax.ppermute(value, axis, [(source, source + steps) for source in range(initial, last)])


def swapped(x, axis, stride):
    return lax.ppermute(x, axis, [(i, i ^ 1 << stride) for i in range(lax.axis_size(axis))])


def normalize(values, gain):
    return values * lax.rsqrt(jnp.mean(values * values, axis=-1, keepdims=True) + 1e-06) * gain


def matmul(left, right):
    return jnp.dot(left, right, preferred_element_type=jnp.float32)


def local(
    seq_in,
    conv_norm,
    conv_weight,
    ff_norm,
    up_weight,
    down_weight,
    head_norm,
    value_weight,
    gate_weight,
    out_weight,
):
    state = seq_in[0].astype(jnp.float32)
    seq_count = lax.axis_size("seq")
    for block in range(conv_weight.shape[0]):
        reach = min(2**block, seq_count // 2)
        normed = normalize(state, conv_norm[block]).astype(jnp.bfloat16)
        before = passed_along(normed, "seq", reach)
        after = passed_along(normed, "seq", -reach)
        piece = lax.all_gather(conv_weight[block], ("seq", "chan"), axis=2, tiled=True)
        total = matmul(before, piece[0]) + matmul(normed, piece[1]) + matmul(after, piece[2])
        conv = total.astype(jnp.bfloat16)
        state = state + conv.astype(jnp.float32)
        mixed = normalize(state, ff_norm[block]).astype(jnp.bfloat16)
        hidden = jax.nn.gelu(
            matmul(mixed, lax.all_gather(up_weight[block], ("seq", "chan"), axis=1, tiled=True))
        ).astype(jnp.bfloat16)
        state = state + matmul(
            hidden, lax.all_gather(down_weight[block], ("seq", "chan"), axis=0, tiled=True)
        )
    final = normalize(state, head_norm).astype(jnp.bfloat16)
    value = matmul(final, value_weight)
    bit_count = (seq_count * lax.axis_size("chan")).bit_length() - 1
    opposite = swapped(final, "strand", 0)
    for digit in range(bit_count):
        opposite = swapped(opposite, ("seq", "chan"), digit)
    opposite = jnp.flip(opposite, 0)
    mirrored = matmul(opposite, gate_weight).astype(jnp.bfloat16)
    gated = (value * jax.nn.sigmoid(mirrored.astype(jnp.float32))).astype(jnp.bfloat16)
    result = matmul(gated, out_weight)
    return result.astype(jnp.bfloat16)[None]


def solution(mesh):
    in_specs = (
        P("strand", ("groups", "seq", "chan"), None),
        P(),
        P(None, None, None, ("seq", "chan")),
        P(),
        P(None, None, ("seq", "chan")),
        P(None, ("seq", "chan"), None),
        P(),
        P(),
        P(),
        P(),
    )
    out_specs = P("strand", ("groups", "seq", "chan"), None)
    return jax.shard_map(local, mesh=mesh, in_specs=in_specs, out_specs=out_specs, check_vma=False)
```

profile of v0, /device:TPU:0, one launch (start us, length us, event | category | flops | bytes accessed | tf_op | source)
XLA Modules:
  0.0 376.3 jit_solution(10085259237027235437)
XLA Ops:
  6.6 1.9 fusion.86
  8.6 1.9 fusion.84
  14.3 5.6 %collective-permute-start = (bf16[384,512]{1,0:T(8,128)(2,1)S(1)}, bf16[384,512]{1,0:T(8,128)(2,1)S(1)}, u32[]{:S(2)}, u32[]{:S(2)}) collective-permute-start(bf16[384,512]{1,0:T(8,128)(2,1)S(1)} %fusion.57), channel_id=1, source_target_pairs={{0,4},{4,8},{8,12},{1,5},{5,9},{9,13},{2,6},{6,10},{10,14},{3,7},{... | collective-permute-start | bytes 1179656 | tf_op jit(solution)/shard_map/ppermute | solution.py:10
  19.9 10.7 %collective-permute-done.1 = bf16[384,512]{1,0:T(8,128)(2,1)S(1)} collective-permute-done((bf16[384,512]{1,0:T(8,128)(2,1)S(1)}, bf16[384,512]{1,0:T(8,128)(2,1)S(1)}, u32[]{:S(2)}, u32[]{:S(2)}) %collective-permute-start.1) | collective-permute-done | bytes 393248 | tf_op jit(solution)/shard_map/ppermute | solution.py:10
  30.6 28.5 %all-gather.13.cloned.1.call-done = bf16[1,3,512,512]{2,3,1,0:T(8,128)(2,1)} async-done(((bf16[1,3,512,64]{2,3,1,0:T(8,128)(2,1)}), bf16[1,3,512,512]{2,3,1,0:T(8,128)(2,1)}) %all-gather.13.cloned.1.call-update) | async-done | bytes 1572880 | tf_op jit(solution)/shard_map/all_gather | solution.py:44
  59.0 1.4 fusion.62
  60.5 1.5 fusion.63
  62.0 1.6 multiply_reduce_fusion.3
  63.6 47.5 %all-gather.15.cloned.1.call-done = bf16[1,512,2048]{2,1,0:T(8,128)(2,1)} async-done(((bf16[1,512,256]{2,1,0:T(8,128)(2,1)}), bf16[1,512,2048]{2,1,0:T(8,128)(2,1)}) %all-gather.15.cloned.1.call-update) | async-done | bytes 2097168 | tf_op jit(solution)/shard_map/all_gather | solution.py:50
  111.0 49.6 %all-gather.17.cloned.1.call-done = bf16[1,2048,512]{2,1,0:T(8,128)(2,1)} async-done(((bf16[1,256,512]{2,1,0:T(8,128)(2,1)}), bf16[1,2048,512]{2,1,0:T(8,128)(2,1)}) %all-gather.17.cloned.1.call-update) | async-done | bytes 2097168 | tf_op jit(solution)/shard_map/all_gather | solution.py:53
  160.7 4.4 %multiply_reduce_fusion.2 = (f32[384]{0:T(512)S(1)}, f32[384,512]{1,0:T(8,128)S(1)}) fusion(f32[384,512]{1,0:T(8,128)S(1)} %get-tuple-element.16, bf16[1,2048,512]{2,1,0:T(8,128)(2,1)} %all-gather.17.cloned.1.call-done, bf16[1,512,2048]{2,1,0:T(8,128)(2,1)} %all-gather.15.cloned.1.call-done, f32[512]{0:T(512)S(1)} %bitcast.91, f32[384]{0:T(512)S(1)} %add_rsqrt_fusion.3), kind=kOutput, calls=%fused_computation.62 | convolution fusion | flops 1618869888 | bytes 5772288 | tf_op jit(solution)/shard_map/dot_general | solution.py:22
  166.5 5.5 %collective-permute-start.2 = (bf16[384,512]{1,0:T(8,128)(2,1)S(1)}, bf16[384,512]{1,0:T(8,128)(2,1)S(1)}, u32[]{:S(2)}, u32[]{:S(2)}) collective-permute-start(bf16[384,512]{1,0:T(8,128)(2,1)S(1)} %multiply_convert_fusion.4), channel_id=1, source_target_pairs={{0,8},{4,12},{1,9},{5,13},{2,10},{6,14},{3,11},{7,15},{16,24},{20,... | collective-permute-start | bytes 1179656 | tf_op jit(solution)/shard_map/ppermute | solution.py:10
  172.0 46.6 %all-gather.19.cloned.1.call-done = bf16[1,3,512,512]{2,3,1,0:T(8,128)(2,1)} async-done(((bf16[1,3,512,64]{2,3,1,0:T(8,128)(2,1)}), bf16[1,3,512,512]{2,3,1,0:T(8,128)(2,1)}) %all-gather.19.cloned.1.call-update) | async-done | bytes 1572880 | tf_op jit(solution)/shard_map/all_gather | solution.py:44
  218.6 1.4 fusion.61
  221.5 1.6 multiply_reduce_fusion.1
  223.1 47.3 %all-gather.21.cloned.1.call-done = bf16[1,512,2048]{2,1,0:T(8,128)(2,1)} async-done(((bf16[1,512,256]{2,1,0:T(8,128)(2,1)}), bf16[1,512,2048]{2,1,0:T(8,128)(2,1)}) %all-gather.21.cloned.1.call-update) | async-done | bytes 2097168 | tf_op jit(solution)/shard_map/all_gather | solution.py:50
  270.4 49.5 %all-gather.23.cloned.1.call-done = bf16[1,2048,512]{2,1,0:T(8,128)(2,1)} async-done(((bf16[1,256,512]{2,1,0:T(8,128)(2,1)}), bf16[1,2048,512]{2,1,0:T(8,128)(2,1)}) %all-gather.23.cloned.1.call-update) | async-done | bytes 2097168 | tf_op jit(solution)/shard_map/all_gather | solution.py:53
  319.9 4.4 %multiply_reduce_fusion = (f32[384]{0:T(512)S(1)}, f32[384,512]{1,0:T(8,128)S(1)}) fusion(f32[384,512]{1,0:T(8,128)S(1)} %get-tuple-element.20, bf16[1,2048,512]{2,1,0:T(8,128)(2,1)} %all-gather.23.cloned.1.call-done, bf16[1,512,2048]{2,1,0:T(8,128)(2,1)} %all-gather.21.cloned.1.call-done, f32[512]{0:T(512)S(1)} %bitcast.90, f32[384]{0:T(512)S(1)} %add_rsqrt_fusion.1), kind=kOutput, calls=%fused_computation.58 | convolution fusion | flops 1618869888 | bytes 5772288 | tf_op jit(solution)/shard_map/dot_general | solution.py:22
  324.5 1.7 collective-permute-done.4
  326.8 10.6 %collective-permute-done.5 = bf16[384,512]{1,0:T(8,128)(2,1)S(1)} collective-permute-done((bf16[384,512]{1,0:T(8,128)(2,1)S(1)}, bf16[384,512]{1,0:T(8,128)(2,1)S(1)}, u32[]{:S(2)}, u32[]{:S(2)}) %collective-permute-start.5) | collective-permute-done | bytes 393248 | tf_op jit(solution)/shard_map/ppermute | solution.py:14
  337.4 1.5 collective-permute-start.6
  338.8 8.8 %collective-permute-done.6 = bf16[384,512]{1,0:T(8,128)(2,1)S(1)} collective-permute-done((bf16[384,512]{1,0:T(8,128)(2,1)S(1)}, bf16[384,512]{1,0:T(8,128)(2,1)S(1)}, u32[]{:S(2)}, u32[]{:S(2)}) %collective-permute-start.6) | collective-permute-done | bytes 393248 | tf_op jit(solution)/shard_map/ppermute | solution.py:14
  347.7 1.8 collective-permute-start.7
  349.5 16.9 %collective-permute-done.7 = bf16[384,512]{1,0:T(8,128)(2,1)S(1)} collective-permute-done((bf16[384,512]{1,0:T(8,128)(2,1)S(1)}, bf16[384,512]{1,0:T(8,128)(2,1)S(1)}, u32[]{:S(2)}, u32[]{:S(2)}) %collective-permute-start.7) | collective-permute-done | bytes 393248 | tf_op jit(solution)/shard_map/ppermute | solution.py:14
  (51 shorter events, 10.5 us)
Async XLA Ops:
  6.5 360.4 %copy-start = (bf16[512,512]{1,0:T(8,128)(2,1)S(1)}, bf16[512,512]{1,0:T(8,128)(2,1)}, u32[]{:S(2)}) copy-start(bf16[512,512]{1,0:T(8,128)(2,1)} %param.18) | copy-start | bytes 1572868
  6.5 4.0 %copy-start.4 = (bf16[2,256,512]{2,1,0:T(8,128)(2,1)S(1)}, bf16[2,256,512]{2,1,0:T(8,128)(2,1)}, u32[]{:S(2)}) copy-start(bf16[2,256,512]{2,1,0:T(8,128)(2,1)} %param.15) | copy-start | bytes 1572868
  6.5 6.1 %copy-start.1 = (bf16[1,384,512]{2,1,0:T(8,128)(2,1)S(1)}, bf16[1,384,512]{2,1,0:T(8,128)(2,1)}, u32[]{:S(2)}) copy-start(bf16[1,384,512]{2,1,0:T(8,128)(2,1)} %param.10) | copy-start | bytes 1179652
  6.5 6.2 %copy-start.5 = (f32[2,512]{1,0:T(2,128)S(1)}, f32[2,512]{1,0:T(2,128)}, u32[]{:S(2)}) copy-start(f32[2,512]{1,0:T(2,128)} %param.11) | copy-start | bytes 12292
  6.5 52.5 %all-gather.13.cloned.1.call-start = ((), (), s32[]{:S(2)}) async-start(), calls=%async_computation | async-start | bytes 1769472 | tf_op jit(solution)/shard_map/all_gather | solution.py:44
  8.5 11.3 %copy-start.6 = (f32[2,512]{1,0:T(2,128)S(1)}, f32[2,512]{1,0:T(2,128)}, u32[]{:S(2)}) copy-start(f32[2,512]{1,0:T(2,128)} %param.13) | copy-start | bytes 12292
  8.5 102.5 %all-gather.15.cloned.1.call-start = ((), (), s32[]{:S(2)}) async-start(), calls=%async_computation.1 | async-start | bytes 2359296 | tf_op jit(solution)/shard_map/all_gather | solution.py:50
  10.5 150.2 %all-gather.17.cloned.1.call-start = ((), (), s32[]{:S(2)}) async-start(), calls=%async_computation.2 | async-start | bytes 2359296 | tf_op jit(solution)/shard_map/all_gather | solution.py:53
  11.4 207.2 %all-gather.19.cloned.1.call-start = ((), (), s32[]{:S(2)}) async-start(), calls=%async_computation.3 | async-start | bytes 1769472 | tf_op jit(solution)/shard_map/all_gather | solution.py:44
  12.0 258.4 %all-gather.21.cloned.1.call-start = ((), (), s32[]{:S(2)}) async-start(), calls=%async_computation.4 | async-start | bytes 2359296 | tf_op jit(solution)/shard_map/all_gather | solution.py:50
  12.6 307.3 %all-gather.23.cloned.1.call-start = ((), (), s32[]{:S(2)}) async-start(), calls=%async_computation.5 | async-start | bytes 2359296 | tf_op jit(solution)/shard_map/all_gather | solution.py:53
  13.0 17.6 %collective-permute-start.1 = (bf16[384,512]{1,0:T(8,128)(2,1)S(1)}, bf16[384,512]{1,0:T(8,128)(2,1)S(1)}, u32[]{:S(2)}, u32[]{:S(2)}) collective-permute-start(bf16[384,512]{1,0:T(8,128)(2,1)S(1)} %fusion.57), channel_id=1, source_target_pairs={{4,0},{8,4},{12,8},{5,1},{9,5},{13,9},{6,2},{10,6},{14,10},{7,3},{... | collective-permute-start | bytes 1179656 | tf_op jit(solution)/shard_map/ppermute | solution.py:10
  14.3 47.7 %collective-permute-start = (bf16[384,512]{1,0:T(8,128)(2,1)S(1)}, bf16[384,512]{1,0:T(8,128)(2,1)S(1)}, u32[]{:S(2)}, u32[]{:S(2)}) collective-permute-start(bf16[384,512]{1,0:T(8,128)(2,1)S(1)} %fusion.57), channel_id=1, source_target_pairs={{0,4},{4,8},{8,12},{1,5},{5,9},{9,13},{2,6},{6,10},{10,14},{3,7},{... | collective-permute-start | bytes 1179656 | tf_op jit(solution)/shard_map/ppermute | solution.py:10
  165.2 54.9 %collective-permute-start.3 = (bf16[384,512]{1,0:T(8,128)(2,1)S(1)}, bf16[384,512]{1,0:T(8,128)(2,1)S(1)}, u32[]{:S(2)}, u32[]{:S(2)}) collective-permute-start(bf16[384,512]{1,0:T(8,128)(2,1)S(1)} %multiply_convert_fusion.4), channel_id=1, source_target_pairs={{8,0},{12,4},{9,1},{13,5},{10,2},{14,6},{11,3},{15,7},{24,16},{28,... | collective-permute-start | bytes 1179656 | tf_op jit(solution)/shard_map/ppermute | solution.py:10
  166.5 55.0 %collective-permute-start.2 = (bf16[384,512]{1,0:T(8,128)(2,1)S(1)}, bf16[384,512]{1,0:T(8,128)(2,1)S(1)}, u32[]{:S(2)}, u32[]{:S(2)}) collective-permute-start(bf16[384,512]{1,0:T(8,128)(2,1)S(1)} %multiply_convert_fusion.4), channel_id=1, source_target_pairs={{0,8},{4,12},{1,9},{5,13},{2,10},{6,14},{3,11},{7,15},{16,24},{20,... | collective-permute-start | bytes 1179656 | tf_op jit(solution)/shard_map/ppermute | solution.py:10
  319.9 4.4 %copy-start.7 = (f32[512]{0:T(512)S(1)}, f32[512]{0:T(512)}, u32[]{:S(2)}) copy-start(f32[512]{0:T(512)} %param.16) | copy-start | bytes 6148
  324.4 1.8 collective-permute-start.4
  326.2 11.2 %collective-permute-start.5 = (bf16[384,512]{1,0:T(8,128)(2,1)S(1)}, bf16[384,512]{1,0:T(8,128)(2,1)S(1)}, u32[]{:S(2)}, u32[]{:S(2)}) collective-permute-start(bf16[384,512]{1,0:T(8,128)(2,1)S(1)} %collective-permute-done.4), channel_id=1, source_target_pairs={{0,1},{1,0},{4,5},{5,4},{8,9},{9,8},{12,13},{13,12},{2,3},{3,2},{6... | collective-permute-start | bytes 1179656 | tf_op jit(solution)/shard_map/ppermute | solution.py:14
  337.4 10.3 %collective-permute-start.6 = (bf16[384,512]{1,0:T(8,128)(2,1)S(1)}, bf16[384,512]{1,0:T(8,128)(2,1)S(1)}, u32[]{:S(2)}, u32[]{:S(2)}) collective-permute-start(bf16[384,512]{1,0:T(8,128)(2,1)S(1)} %collective-permute-done.5), channel_id=1, source_target_pairs={{0,4},{1,5},{4,0},{5,1},{8,12},{9,13},{12,8},{13,9},{2,6},{3,7},{6... | collective-permute-start | bytes 1179656 | tf_op jit(solution)/shard_map/ppermute | solution.py:14
  347.7 18.7 %collective-permute-start.7 = (bf16[384,512]{1,0:T(8,128)(2,1)S(1)}, bf16[384,512]{1,0:T(8,128)(2,1)S(1)}, u32[]{:S(2)}, u32[]{:S(2)}) collective-permute-start(bf16[384,512]{1,0:T(8,128)(2,1)S(1)} %collective-permute-done.6), channel_id=1, source_target_pairs={{0,8},{1,9},{4,12},{5,13},{8,0},{9,1},{12,4},{13,5},{2,10},{3,11},... | collective-permute-start | bytes 1179656 | tf_op jit(solution)/shard_map/ppermute | solution.py:14
  366.9 1.0 copy-start.2
  366.9 1.2 copy-start.3
Sparse Core Ops, SparseCore 0:
  9.6 49.4 all-gather.12
  61.1 49.8 all-gather.14
  113.1 47.4 all-gather.16
  162.7 55.8 all-gather.18
  220.5 49.8 all-gather.20
  272.4 47.4 all-gather.22
where the time goes:
time: 377 us; the launch traced here: 376 us
  waiting for transfers between devices  319 us (85%)
  matrix products  19.5 us (5%)
  starting transfers between devices  17.8 us (5%)
  between operations  13.7 us (4%)
  local copies, waits for them, and re-layouts  5.8 us (2%)
    all_gather x2, waiting for transfers between devices, local(): lax.all_gather(down_weight[block], ('seq', 'chan'), axis=0, tiled=True)  99.1 us
    all_gather x2, waiting for transfers between devices, local(): lax.all_gather(up_weight[block], ('seq', 'chan'), axis=1, tiled=True)  94.8 us
    all_gather x2, waiting for transfers between devices, local(): lax.all_gather(conv_weight[block], ('seq', 'chan'), axis=2, tiled=True)  75.1 us
    ppermute x4, waiting for transfers between devices, swapped(): lax.ppermute(x, axis, [(i, i ^ 1 << stride) for i in range(lax.axis_size(...  38.1 us
    dot_general x10, matrix products, matmul(): return jnp.dot(left, right, preferred_element_type=jnp.float32)  19.5 us
    ppermute x4, starting transfers between devices, passed_along(): lax.ppermute(value, axis, [(source, source + steps) for source in range(i...  13.7 us
    ppermute x4, waiting for transfers between devices, passed_along(): lax.ppermute(value, axis, [(source, source + steps) for source in range(i...  10.7 us
  transfers between devices with their start and end apart: 14, of which 11 were waited for; matrix products, arithmetic and copies ran while one was open for 4% of the time, Pallas kernels for 0%

commit v1 on v0

--- a/solution.py
+++ b/solution.py
@@ -2,6 +2,28 @@
 import jax.numpy as jnp
 from jax import lax
 from jax.sharding import PartitionSpec as P
+
+
+def laid_out(parts, dim):
+    parts = jnp.moveaxis(parts, 0, dim)
+    dims = parts.shape
+    return parts.reshape(*dims[:dim], dims[dim] * dims[dim + 1], *dims[dim + 2 :])
+
+
+def gather_around(x, axis, dim):
+    devices = lax.axis_size(axis)
+    pairs = [(i, (i + 1) % devices) for i in range(devices)]
+    back = [(b, a) for a, b in pairs]
+    lower, upper = ([], [])
+    for step in range(devices - 1):
+        if step % 2 == 0:
+            lower.append(lax.ppermute(lower[-1] if lower else x, axis, pairs))
+        else:
+            upper.append(lax.ppermute(upper[-1] if upper else x, axis, back))
+    blocks = jnp.stack([*lower[::-1], x, *upper])
+    shift = lax.axis_index(axis) - len(lower)
+    blocks = blocks[(jnp.arange(devices) - shift) % devices]
+    return laid_out(blocks, dim)
 
 
 def passed_along(value, axis, steps):
@@ -41,7 +63,7 @@
         normed = normalize(state, conv_norm[block]).astype(jnp.bfloat16)
         before = passed_along(normed, "seq", reach)
         after = passed_along(normed, "seq", -reach)
-        piece = lax.all_gather(conv_weight[block], ("seq", "chan"), axis=2, tiled=True)
+        piece = gather_around(conv_weight[block], ("seq", "chan"), 2)
         total = matmul(before, piece[0]) + matmul(normed, piece[1]) + matmul(after, piece[2])
         conv = total.astype(jnp.bfloat16)
         state = state + conv.astype(jnp.float32)

time: 377 us -> 314 us (0.83)
  waiting for transfers between devices: 319 us -> 220 us
  starting transfers between devices: 17.8 us -> 40.2 us
  local copies, waits for them, and re-layouts: 5.8 us -> 20.9 us
    all_gather x2 -> x0, waiting for transfers between devices: 75.1 us -> none  [local(): lax.all_gather(conv_weight[block], ('seq', 'chan'), axis=2, tiled=True)]
    all_gather x2, waiting for transfers between devices: 99.1 us -> 49.5 us  [local(): lax.all_gather(down_weight[block], ('seq', 'chan'), axis=0, tiled=True)]
    ppermute x0 -> x14, waiting for transfers between devices: none -> 46.2 us  [the longest x8 46.1 us: gather_around(): lower.append(lax.ppermute(lower[-1] if lower else x, axis, pairs))]
    all_gather x2, waiting for transfers between devices: 94.8 us -> 64.4 us  [local(): lax.all_gather(up_weight[block], ('seq', 'chan'), axis=1, tiled=True)]
    ppermute x0 -> x14, starting transfers between devices: none -> 26 us  [the longest x6 18.5 us: gather_around(): upper.append(lax.ppermute(upper[-1] if upper else x, axis, back))]
    ppermute x4, waiting for transfers between devices: 10.7 us -> 21.6 us  [passed_along(): lax.ppermute(value, axis, [(source, source + steps) for source in range(i...]
    unnamed x16 -> x33, local copies, waits for them, and re-layouts: 0.73 us -> 9.85 us
    gather x0 -> x2, local copies, waits for them, and re-layouts: none -> 4.17 us  [gather_around(): blocks = blocks[(jnp.arange(devices) - shift) % devices]]
  transfers between devices with their start and end apart: 14 -> 26, of which waited for: 11 -> 14; matrix products, arithmetic and copies ran while one was open for 4% -> 10% of each run, Pallas kernels for 0% -> 0%
where the time goes in v1:
time: 314 us
  waiting for transfers between devices  220 us (70%)
  starting transfers between devices  40.2 us (13%)
  local copies, waits for them, and re-layouts  20.9 us (7%)
  matrix products  17.6 us (6%)
  between operations  13.4 us (4%)
    all_gather x2, waiting for transfers between devices, local(): lax.all_gather(up_weight[block], ('seq', 'chan'), axis=1, tiled=True)  64.4 us
    all_gather x2, waiting for transfers between devices, local(): lax.all_gather(down_weight[block], ('seq', 'chan'), axis=0, tiled=True)  49.5 us
    ppermute x8, waiting for transfers between devices, gather_around(): lower.append(lax.ppermute(lower[-1] if lower else x, axis, pairs))  46.1 us
    ppermute x4, waiting for transfers between devices, swapped(): lax.ppermute(x, axis, [(i, i ^ 1 << stride) for i in range(lax.axis_size(...  38.1 us
    ppermute x4, waiting for transfers between devices, passed_along(): lax.ppermute(value, axis, [(source, source + steps) for source in range(i...  21.6 us
    ppermute x6, starting transfers between devices, gather_around(): upper.append(lax.ppermute(upper[-1] if upper else x, axis, back))  18.5 us
    dot_general x10, matrix products, matmul(): return jnp.dot(left, right, preferred_element_type=jnp.float32)  17.6 us
    ppermute x4, starting transfers between devices, passed_along(): lax.ppermute(value, axis, [(source, source + steps) for source in range(i...  10.1 us
  transfers between devices with their start and end apart: 26, of which 14 were waited for; matrix products, arithmetic and copies ran while one was open for 10% of the time, Pallas kernels for 0%

profile of v1, /device:TPU:0, one launch (start us, length us, event | category | flops | bytes accessed | tf_op | source)
XLA Modules:
  0.0 313.9 jit_solution(6227814277452824533)
XLA Ops:
  10.3 3.0 collective-permute-start.1
  13.3 3.1 collective-permute-start.5
  16.4 4.7 %collective-permute-start.14 = (bf16[3,512,64]{1,2,0:T(8,128)(2,1)S(1)}, bf16[3,512,64]{1,2,0:T(8,128)(2,1)S(1)}, u32[]{:S(2)}, u32[]{:S(2)}) collective-permute-start(bf16[3,512,64]{1,2,0:T(8,128)(2,1)S(1)} %get-tuple-element.17), channel_id=1, source_target_pairs={{1,0},{4,1},{5,4},{8,5},{9,8},{12,9},{13,12},{0,13},{3,2},{6,3},{7... | collective-permute-start | bytes 589832 | tf_op jit(solution)/shard_map/ppermute | solution.py:22
  21.3 8.5 %collective-permute-done.1 = bf16[3,512,64]{1,2,0:T(8,128)(2,1)S(1)} collective-permute-done((bf16[3,512,64]{1,2,0:T(8,128)(2,1)S(1)}, bf16[3,512,64]{1,2,0:T(8,128)(2,1)S(1)}, u32[]{:S(2)}, u32[]{:S(2)}) %collective-permute-start.1) | collective-permute-done | bytes 196640 | tf_op jit(solution)/shard_map/ppermute | solution.py:20
  29.9 2.5 collective-permute-start.2
  36.6 7.8 %collective-permute-done.2 = bf16[3,512,64]{1,2,0:T(8,128)(2,1)S(1)} collective-permute-done((bf16[3,512,64]{1,2,0:T(8,128)(2,1)S(1)}, bf16[3,512,64]{1,2,0:T(8,128)(2,1)S(1)}, u32[]{:S(2)}, u32[]{:S(2)}) %collective-permute-start.2) | collective-permute-done | bytes 196640 | tf_op jit(solution)/shard_map/ppermute | solution.py:20
  44.4 4.8 %collective-permute-start.6 = (bf16[3,512,64]{1,2,0:T(8,128)(2,1)S(1)}, bf16[3,512,64]{1,2,0:T(8,128)(2,1)S(1)}, u32[]{:S(2)}, u32[]{:S(2)}) collective-permute-start(bf16[3,512,64]{1,2,0:T(8,128)(2,1)S(1)} %collective-permute-done.5), channel_id=1, source_target_pairs={{1,0},{4,1},{5,4},{8,5},{9,8},{12,9},{13,12},{0,13},{3,2},{6,3},{7... | collective-permute-start | bytes 589832 | tf_op jit(solution)/shard_map/ppermute | solution.py:22
  49.2 12.6 %collective-permute-done.11 = bf16[3,512,64]{1,2,0:T(8,128)(2,1)S(1)} collective-permute-done((bf16[3,512,64]{1,2,0:T(8,128)(2,1)S(1)}, bf16[3,512,64]{1,2,0:T(8,128)(2,1)S(1)}, u32[]{:S(2)}, u32[]{:S(2)}) %collective-permute-start.11) | collective-permute-done | bytes 196640 | tf_op jit(solution)/shard_map/ppermute | solution.py:20
  61.8 7.9 %collective-permute-done.3 = bf16[3,512,64]{1,2,0:T(8,128)(2,1)S(1)} collective-permute-done((bf16[3,512,64]{1,2,0:T(8,128)(2,1)S(1)}, bf16[3,512,64]{1,2,0:T(8,128)(2,1)S(1)}, u32[]{:S(2)}, u32[]{:S(2)}) %collective-permute-start.3) | collective-permute-done | bytes 196640 | tf_op jit(solution)/shard_map/ppermute | solution.py:20
  69.7 2.1 collective-permute-start
  71.8 4.0 %collective-permute-start.7 = (bf16[3,512,64]{1,2,0:T(8,128)(2,1)S(1)}, bf16[3,512,64]{1,2,0:T(8,128)(2,1)S(1)}, u32[]{:S(2)}, u32[]{:S(2)}) collective-permute-start(bf16[3,512,64]{1,2,0:T(8,128)(2,1)S(1)} %collective-permute-done.6), channel_id=1, source_target_pairs={{1,0},{4,1},{5,4},{8,5},{9,8},{12,9},{13,12},{0,13},{3,2},{6,3},{7... | collective-permute-start | bytes 589832 | tf_op jit(solution)/shard_map/ppermute | solution.py:22
  81.3 8.5 %collective-permute-done.13 = bf16[3,512,64]{1,2,0:T(8,128)(2,1)S(1)} collective-permute-done((bf16[3,512,64]{1,2,0:T(8,128)(2,1)S(1)}, bf16[3,512,64]{1,2,0:T(8,128)(2,1)S(1)}, u32[]{:S(2)}, u32[]{:S(2)}) %collective-permute-start.13) | collective-permute-done | bytes 196640 | tf_op jit(solution)/shard_map/ppermute | solution.py:20
  103.0 2.1 gather_fusion.1
  106.7 2.4 multiply_reduce_fusion.3
  109.1 38.4 %all-gather.9.cloned.1.call-done = bf16[1,512,2048]{2,1,0:T(8,128)(2,1)} async-done(((bf16[1,512,256]{2,1,0:T(8,128)(2,1)}), bf16[1,512,2048]{2,1,0:T(8,128)(2,1)}) %all-gather.9.cloned.1.call-update) | async-done | bytes 2097168 | tf_op jit(solution)/shard_map/all_gather | solution.py:72
  147.4 4.8 %multiply_reduce_fusion.2 = (f32[384]{0:T(512)S(1)}, f32[384,512]{1,0:T(8,128)S(1)}) fusion(f32[384,512]{1,0:T(8,128)} %get-tuple-element.24, bf16[1,2048,512]{2,1,0:T(8,128)(2,1)} %all-gather.11.cloned.1.call-done, bf16[1,512,2048]{2,1,0:T(8,128)(2,1)} %all-gather.9.cloned.1.call-done, f32[512]{0:T(512)S(1)} %bitcast.125, f32[384]{0:T(512)S(1)} %add_rsqrt_fusion.3), kind=kOutput, calls=%fused_computation.64 | convolution fusion | flops 1618869888 | bytes 5772288 | tf_op jit(solution)/shard_map/dot_general | solution.py:44
  153.8 5.5 %collective-permute-start.9 = (bf16[384,512]{1,0:T(8,128)(2,1)S(1)}, bf16[384,512]{1,0:T(8,128)(2,1)S(1)}, u32[]{:S(2)}, u32[]{:S(2)}) collective-permute-start(bf16[384,512]{1,0:T(8,128)(2,1)S(1)} %multiply_convert_fusion.4), channel_id=1, source_target_pairs={{0,8},{4,12},{1,9},{5,13},{2,10},{6,14},{3,11},{7,15},{16,24},{20,... | collective-permute-start | bytes 1179656 | tf_op jit(solution)/shard_map/ppermute | solution.py:32
  159.7 21.6 %collective-permute-done.17 = bf16[384,512]{1,0:T(8,128)(2,1)S(1)} collective-permute-done((bf16[384,512]{1,0:T(8,128)(2,1)S(1)}, bf16[384,512]{1,0:T(8,128)(2,1)S(1)}, u32[]{:S(2)}, u32[]{:S(2)}) %collective-permute-start.17) | collective-permute-done | bytes 393248 | tf_op jit(solution)/shard_map/ppermute | solution.py:32
  182.3 26.0 %all-gather.13.cloned.1.call-done = bf16[1,512,2048]{2,1,0:T(8,128)(2,1)} async-done(((bf16[1,512,256]{2,1,0:T(8,128)(2,1)}), bf16[1,512,2048]{2,1,0:T(8,128)(2,1)}) %all-gather.13.cloned.1.call-update) | async-done | bytes 2097168 | tf_op jit(solution)/shard_map/all_gather | solution.py:72
  208.3 49.5 %all-gather.15.cloned.1.call-done = bf16[1,2048,512]{2,1,0:T(8,128)(2,1)} async-done(((bf16[1,256,512]{2,1,0:T(8,128)(2,1)}), bf16[1,2048,512]{2,1,0:T(8,128)(2,1)}) %all-gather.15.cloned.1.call-update) | async-done | bytes 2097168 | tf_op jit(solution)/shard_map/all_gather | solution.py:75
  257.8 4.4 %multiply_reduce_fusion = (f32[384]{0:T(512)S(1)}, f32[384,512]{1,0:T(8,128)S(1)}) fusion(f32[384,512]{1,0:T(8,128)S(1)} %get-tuple-element.28, bf16[1,2048,512]{2,1,0:T(8,128)(2,1)} %all-gather.15.cloned.1.call-done, bf16[1,512,2048]{2,1,0:T(8,128)(2,1)} %all-gather.13.cloned.1.call-done, f32[512]{0:T(512)S(1)} %bitcast.124, f32[384]{0:T(512)S(1)} %add_rsqrt_fusion.1), kind=kOutput, calls=%fused_computation.60 | convolution fusion | flops 1618869888 | bytes 5772288 | tf_op jit(solution)/shard_map/dot_general | solution.py:44
  264.7 10.6 %collective-permute-done.19 = bf16[384,512]{1,0:T(8,128)(2,1)S(1)} collective-permute-done((bf16[384,512]{1,0:T(8,128)(2,1)S(1)}, bf16[384,512]{1,0:T(8,128)(2,1)S(1)}, u32[]{:S(2)}, u32[]{:S(2)}) %collective-permute-start.19) | collective-permute-done | bytes 393248 | tf_op jit(solution)/shard_map/ppermute | solution.py:36
  276.8 8.8 %collective-permute-done.20 = bf16[384,512]{1,0:T(8,128)(2,1)S(1)} collective-permute-done((bf16[384,512]{1,0:T(8,128)(2,1)S(1)}, bf16[384,512]{1,0:T(8,128)(2,1)S(1)}, u32[]{:S(2)}, u32[]{:S(2)}) %collective-permute-start.20) | collective-permute-done | bytes 393248 | tf_op jit(solution)/shard_map/ppermute | solution.py:36
  287.4 16.9 %collective-permute-done.21 = bf16[384,512]{1,0:T(8,128)(2,1)S(1)} collective-permute-done((bf16[384,512]{1,0:T(8,128)(2,1)S(1)}, bf16[384,512]{1,0:T(8,128)(2,1)S(1)}, u32[]{:S(2)}, u32[]{:S(2)}) %collective-permute-start.21) | collective-permute-done | bytes 393248 | tf_op jit(solution)/shard_map/ppermute | solution.py:36
  (98 shorter events, 40.1 us)
Async XLA Ops:
  6.5 102.5 %all-gather.11.cloned.1.call-start = ((), (), s32[]{:S(2)}) async-start(), calls=%async_computation.1 | async-start | bytes 2359296 | tf_op jit(solution)/shard_map/all_gather | solution.py:75
  8.6 138.9 %all-gather.9.cloned.1.call-start = ((), (), s32[]{:S(2)}) async-start(), calls=%async_computation | async-start | bytes 2359296 | tf_op jit(solution)/shard_map/all_gather | solution.py:72
  9.5 198.8 %all-gather.13.cloned.1.call-start = ((), (), s32[]{:S(2)}) async-start(), calls=%async_computation.2 | async-start | bytes 2359296 | tf_op jit(solution)/shard_map/all_gather | solution.py:72
  10.2 247.6 %all-gather.15.cloned.1.call-start = ((), (), s32[]{:S(2)}) async-start(), calls=%async_computation.3 | async-start | bytes 2359296 | tf_op jit(solution)/shard_map/all_gather | solution.py:75
  10.3 19.5 %collective-permute-start.1 = (bf16[3,512,64]{1,2,0:T(8,128)(2,1)S(1)}, bf16[3,512,64]{1,2,0:T(8,128)(2,1)S(1)}, u32[]{:S(2)}, u32[]{:S(2)}) collective-permute-start(bf16[3,512,64]{1,2,0:T(8,128)(2,1)S(1)} %get-tuple-element.18), channel_id=1, source_target_pairs={{0,1},{1,4},{4,5},{5,8},{8,9},{9,12},{12,13},{13,0},{2,3},{3,6},{6... | collective-permute-start | bytes 589832 | tf_op jit(solution)/shard_map/ppermute | solution.py:20
  13.3 31.0 %collective-permute-start.5 = (bf16[3,512,64]{1,2,0:T(8,128)(2,1)S(1)}, bf16[3,512,64]{1,2,0:T(8,128)(2,1)S(1)}, u32[]{:S(2)}, u32[]{:S(2)}) collective-permute-start(bf16[3,512,64]{1,2,0:T(8,128)(2,1)S(1)} %get-tuple-element.18), channel_id=1, source_target_pairs={{1,0},{4,1},{5,4},{8,5},{9,8},{12,9},{13,12},{0,13},{3,2},{6,3},{7... | collective-permute-start | bytes 589832 | tf_op jit(solution)/shard_map/ppermute | solution.py:22
  16.4 18.1 %collective-permute-start.10 = (bf16[3,512,64]{1,2,0:T(8,128)(2,1)S(1)}, bf16[3,512,64]{1,2,0:T(8,128)(2,1)S(1)}, u32[]{:S(2)}, u32[]{:S(2)}) collective-permute-start(bf16[3,512,64]{1,2,0:T(8,128)(2,1)S(1)} %get-tuple-element.17), channel_id=1, source_target_pairs={{0,1},{1,4},{4,5},{5,8},{8,9},{9,12},{12,13},{13,0},{2,3},{3,6},{6... | collective-permute-start | bytes 589832 | tf_op jit(solution)/shard_map/ppermute | solution.py:20
  16.4 32.7 %collective-permute-start.14 = (bf16[3,512,64]{1,2,0:T(8,128)(2,1)S(1)}, bf16[3,512,64]{1,2,0:T(8,128)(2,1)S(1)}, u32[]{:S(2)}, u32[]{:S(2)}) collective-permute-start(bf16[3,512,64]{1,2,0:T(8,128)(2,1)S(1)} %get-tuple-element.17), channel_id=1, source_target_pairs={{1,0},{4,1},{5,4},{8,5},{9,8},{12,9},{13,12},{0,13},{3,2},{6,3},{7... | collective-permute-start | bytes 589832 | tf_op jit(solution)/shard_map/ppermute | solution.py:22
  29.9 14.5 %collective-permute-start.2 = (bf16[3,512,64]{1,2,0:T(8,128)(2,1)S(1)}, bf16[3,512,64]{1,2,0:T(8,128)(2,1)S(1)}, u32[]{:S(2)}, u32[]{:S(2)}) collective-permute-start(bf16[3,512,64]{1,2,0:T(8,128)(2,1)S(1)} %collective-permute-done.1), channel_id=1, source_target_pairs={{0,1},{1,4},{4,5},{5,8},{8,9},{9,12},{12,13},{13,0},{2,3},{3,6},{6... | collective-permute-start | bytes 589832 | tf_op jit(solution)/shard_map/ppermute | solution.py:20
  33.3 66.0 %collective-permute-start.8 = (bf16[384,512]{1,0:T(8,128)(2,1)}, bf16[384,512]{1,0:T(8,128)(2,1)}, u32[]{:S(2)}, u32[]{:S(2)}) collective-permute-start(bf16[384,512]{1,0:T(8,128)(2,1)} %fusion.57), channel_id=1, source_target_pairs={{4,0},{8,4},{12,8},{5,1},{9,5},{13,9},{6,2},{10,6},{14,10},{7,3},{... | collective-permute-start | bytes 1179656 | tf_op jit(solution)/shard_map/ppermute | solution.py:32
  34.6 27.2 %collective-permute-start.11 = (bf16[3,512,64]{1,2,0:T(8,128)(2,1)S(1)}, bf16[3,512,64]{1,2,0:T(8,128)(2,1)S(1)}, u32[]{:S(2)}, u32[]{:S(2)}) collective-permute-start(bf16[3,512,64]{1,2,0:T(8,128)(2,1)S(1)} %collective-permute-done.10), channel_id=1, source_target_pairs={{0,1},{1,4},{4,5},{5,8},{8,9},{9,12},{12,13},{13,0},{2,3},{3,6},{6... | collective-permute-start | bytes 589832 | tf_op jit(solution)/shard_map/ppermute | solution.py:20
  44.3 25.3 %collective-permute-start.3 = (bf16[3,512,64]{1,2,0:T(8,128)(2,1)S(1)}, bf16[3,512,64]{1,2,0:T(8,128)(2,1)S(1)}, u32[]{:S(2)}, u32[]{:S(2)}) collective-permute-start(bf16[3,512,64]{1,2,0:T(8,128)(2,1)S(1)} %collective-permute-done.2), channel_id=1, source_target_pairs={{0,1},{1,4},{4,5},{5,8},{8,9},{9,12},{12,13},{13,0},{2,3},{3,6},{6... | collective-permute-start | bytes 589832 | tf_op jit(solution)/shard_map/ppermute | solution.py:20
  44.4 25.3 %collective-permute-start.6 = (bf16[3,512,64]{1,2,0:T(8,128)(2,1)S(1)}, bf16[3,512,64]{1,2,0:T(8,128)(2,1)S(1)}, u32[]{:S(2)}, u32[]{:S(2)}) collective-permute-start(bf16[3,512,64]{1,2,0:T(8,128)(2,1)S(1)} %collective-permute-done.5), channel_id=1, source_target_pairs={{1,0},{4,1},{5,4},{8,5},{9,8},{12,9},{13,12},{0,13},{3,2},{6,3},{7... | collective-permute-start | bytes 589832 | tf_op jit(solution)/shard_map/ppermute | solution.py:22
  49.1 22.6 %collective-permute-start.15 = (bf16[3,512,64]{1,2,0:T(8,128)(2,1)S(1)}, bf16[3,512,64]{1,2,0:T(8,128)(2,1)S(1)}, u32[]{:S(2)}, u32[]{:S(2)}) collective-permute-start(bf16[3,512,64]{1,2,0:T(8,128)(2,1)S(1)} %collective-permute-done.14), channel_id=1, source_target_pairs={{1,0},{4,1},{5,4},{8,5},{9,8},{12,9},{13,12},{0,13},{3,2},{6,3},{7... | collective-permute-start | bytes 589832 | tf_op jit(solution)/shard_map/ppermute | solution.py:22
  61.8 14.0 %collective-permute-start.12 = (bf16[3,512,64]{1,2,0:T(8,128)(2,1)S(1)}, bf16[3,512,64]{1,2,0:T(8,128)(2,1)S(1)}, u32[]{:S(2)}, u32[]{:S(2)}) collective-permute-start(bf16[3,512,64]{1,2,0:T(8,128)(2,1)S(1)} %collective-permute-done.11), channel_id=1, source_target_pairs={{0,1},{1,4},{4,5},{5,8},{8,9},{9,12},{12,13},{13,0},{2,3},{3,6},{6... | collective-permute-start | bytes 589832 | tf_op jit(solution)/shard_map/ppermute | solution.py:20
  69.7 37.0 %collective-permute-start = (bf16[384,512]{1,0:T(8,128)(2,1)}, bf16[384,512]{1,0:T(8,128)(2,1)}, u32[]{:S(2)}, u32[]{:S(2)}) collective-permute-start(bf16[384,512]{1,0:T(8,128)(2,1)} %fusion.57), channel_id=1, source_target_pairs={{0,4},{4,8},{8,12},{1,5},{5,9},{9,13},{2,6},{6,10},{10,14},{3,7},{... | collective-permute-start | bytes 1179656 | tf_op jit(solution)/shard_map/ppermute | solution.py:32
  71.8 23.7 %collective-permute-start.7 = (bf16[3,512,64]{1,2,0:T(8,128)(2,1)S(1)}, bf16[3,512,64]{1,2,0:T(8,128)(2,1)S(1)}, u32[]{:S(2)}, u32[]{:S(2)}) collective-permute-start(bf16[3,512,64]{1,2,0:T(8,128)(2,1)S(1)} %collective-permute-done.6), channel_id=1, source_target_pairs={{1,0},{4,1},{5,4},{8,5},{9,8},{12,9},{13,12},{0,13},{3,2},{6,3},{7... | collective-permute-start | bytes 589832 | tf_op jit(solution)/shard_map/ppermute | solution.py:22
  75.8 25.6 %collective-permute-start.16 = (bf16[3,512,64]{1,2,0:T(8,128)(2,1)S(1)}, bf16[3,512,64]{1,2,0:T(8,128)(2,1)}, u32[]{:S(2)}, u32[]{:S(2)}) collective-permute-start(bf16[3,512,64]{1,2,0:T(8,128)(2,1)S(1)} %collective-permute-done.15), channel_id=1, source_target_pairs={{1,0},{4,1},{5,4},{8,5},{9,8},{12,9},{13,12},{0,13},{3,2},{6,3},{7... | collective-permute-start | bytes 589832 | tf_op jit(solution)/shard_map/ppermute | solution.py:22
  78.5 11.3 %collective-permute-start.13 = (bf16[3,512,64]{1,2,0:T(8,128)(2,1)S(1)}, bf16[3,512,64]{1,2,0:T(8,128)(2,1)S(1)}, u32[]{:S(2)}, u32[]{:S(2)}) collective-permute-start(bf16[3,512,64]{1,2,0:T(8,128)(2,1)S(1)} %collective-permute-done.12), channel_id=1, source_target_pairs={{0,1},{1,4},{4,5},{5,8},{8,9},{9,12},{12,13},{13,0},{2,3},{3,6},{6... | collective-permute-start | bytes 589832 | tf_op jit(solution)/shard_map/ppermute | solution.py:20
  152.4 28.9 %collective-permute-start.17 = (bf16[384,512]{1,0:T(8,128)(2,1)S(1)}, bf16[384,512]{1,0:T(8,128)(2,1)S(1)}, u32[]{:S(2)}, u32[]{:S(2)}) collective-permute-start(bf16[384,512]{1,0:T(8,128)(2,1)S(1)} %multiply_convert_fusion.4), channel_id=1, source_target_pairs={{8,0},{12,4},{9,1},{13,5},{10,2},{14,6},{11,3},{15,7},{24,16},{28,... | collective-permute-start | bytes 1179656 | tf_op jit(solution)/shard_map/ppermute | solution.py:32
  153.8 27.9 %collective-permute-start.9 = (bf16[384,512]{1,0:T(8,128)(2,1)S(1)}, bf16[384,512]{1,0:T(8,128)(2,1)S(1)}, u32[]{:S(2)}, u32[]{:S(2)}) collective-permute-start(bf16[384,512]{1,0:T(8,128)(2,1)S(1)} %multiply_convert_fusion.4), channel_id=1, source_target_pairs={{0,8},{4,12},{1,9},{5,13},{2,10},{6,14},{3,11},{7,15},{16,24},{20,... | collective-permute-start | bytes 1179656 | tf_op jit(solution)/shard_map/ppermute | solution.py:32
  264.1 11.2 %collective-permute-start.19 = (bf16[384,512]{1,0:T(8,128)(2,1)S(1)}, bf16[384,512]{1,0:T(8,128)(2,1)S(1)}, u32[]{:S(2)}, u32[]{:S(2)}) collective-permute-start(bf16[384,512]{1,0:T(8,128)(2,1)S(1)} %collective-permute-done.18), channel_id=1, source_target_pairs={{0,1},{1,0},{4,5},{5,4},{8,9},{9,8},{12,13},{13,12},{2,3},{3,2},{6... | collective-permute-start | bytes 1179656 | tf_op jit(solution)/shard_map/ppermute | solution.py:36
  275.3 10.3 %collective-permute-start.20 = (bf16[384,512]{1,0:T(8,128)(2,1)S(1)}, bf16[384,512]{1,0:T(8,128)(2,1)S(1)}, u32[]{:S(2)}, u32[]{:S(2)}) collective-permute-start(bf16[384,512]{1,0:T(8,128)(2,1)S(1)} %collective-permute-done.19), channel_id=1, source_target_pairs={{0,4},{1,5},{4,0},{5,1},{8,12},{9,13},{12,8},{13,9},{2,6},{3,7},{6... | collective-permute-start | bytes 1179656 | tf_op jit(solution)/shard_map/ppermute | solution.py:36
  285.6 18.7 %collective-permute-start.21 = (bf16[384,512]{1,0:T(8,128)(2,1)S(1)}, bf16[384,512]{1,0:T(8,128)(2,1)S(1)}, u32[]{:S(2)}, u32[]{:S(2)}) collective-permute-start(bf16[384,512]{1,0:T(8,128)(2,1)S(1)} %collective-permute-done.20), channel_id=1, source_target_pairs={{0,8},{1,9},{4,12},{5,13},{8,0},{9,1},{12,4},{13,5},{2,10},{3,11},... | collective-permute-start | bytes 1179656 | tf_op jit(solution)/shard_map/ppermute | solution.py:36
  (12 other events, 408.5 us)
Sparse Core Ops, SparseCore 0:
  9.5 82.5 all-gather.10
  94.1 53.2 all-gather.8
  149.5 58.7 all-gather.12
  210.3 47.4 all-gather.14
